TPU v7x, 32 devices: a whole 2x2x4 slice. The times are simulated.
32 devices in a mesh: clip: 8 (over z, x), tm: 4 (over y, core).
Axes of the slice: x: 2, y: 2, z: 4, core: 2. Of those that a mesh axis runs over, the one named last changes fastest.
Arguments:
- features: bfloat16 [16, 1024, 512], P('clip', 'tm'), may hold values from -6 to 6
- cotangent: bfloat16 [16, 1024, 512], P('clip', 'tm'), may hold values from -6 to 6
- clip_lengths: int32 [16], P('clip'), may hold values from 128 to 1024, as said below
- code_ids: int32 [4, 16, 1024], P(None, 'clip', 'tm'), may hold values from 0 to 1023
- step_count: int32 [1], replicated, may hold values from 2 to 20
- dilated_kernel_weight: float32 [3, 512, 256], P(None, None, 'clip'), may hold values from -0.15625 to 0.15625
- pointwise_conv: float32 [256, 512], P(None, 'clip'), may hold values from -0.75 to 0.75
- codebooks: float32 [4, 1024, 256], P(None, 'clip'), may hold values from -6 to 6
- dilated_first_moment: float32 [3, 512, 256], P(None, None, 'clip'), may hold values from -1 to 1
- dilated_second_moment: float32 [3, 512, 256], P(None, None, 'clip'), may hold values from 0.028995216 to 0.11598086
- pointwise_first: float32 [256, 512], P(None, 'clip'), may hold values from -1 to 1
- pointwise_second: float32 [256, 512], P(None, 'clip'), may hold values from 0.028995216 to 0.11598086
- codebook_first: float32 [4, 1024, 256], P(None, 'clip'), may hold values from -0.01953125 to 0.01953125
- codebook_second: float32 [4, 1024, 256], P(None, 'clip'), may hold values from 9.745614e-06 to 3.8982456e-05
Outputs:
- quantized: bfloat16 [16, 1024, 512], P('clip', 'tm')
- features_gradient: float32 [16, 1024, 512], P('clip', 'tm')
- grad_norm: float32 [1], replicated
- dilated_new: float32 [3, 512, 256], P(None, None, 'clip')
- dilated_grad: float32 [3, 512, 256], P(None, None, 'clip')
- dilated_square: float32 [3, 512, 256], P(None, None, 'clip')
- pointwise_new: float32 [256, 512], P(None, 'clip')
- pointwise_grad: float32 [256, 512], P(None, 'clip')
- pointwise_square: float32 [256, 512], P(None, 'clip')
- codebook_new: float32 [4, 1024, 256], P(None, 'clip')
- codebook_grad: float32 [4, 1024, 256], P(None, 'clip')
- codebook_square: float32 [4, 1024, 256], P(None, 'clip')
Inputs may be any that keep to these rules, and one draw needn't show every extreme that they name: `clip_lengths`: the number of valid frames of each clip; frames from it on are padding; clip 0 is always full.
All inputs are finite; a program needn't handle non-finite values.
Results may differ from a plain program's by a relative error of at most 0.001.
The roundings to bfloat16 on the way count: a program that leaves them out, or rounds other values in their place, can miss the bound.
Values may be sent and summed in bfloat16 or wider, within the bound.
No kernel may reach another device: no remote copies, remote signals or barrier semaphores. Data moves between devices by JAX's collectives and lax.ppermute only.
A program may use at most 64 MiB of HBM per device.

v0:
```python
import jax
import jax.numpy as jnp
from jax import lax
from jax.sharding import PartitionSpec as P

HID = 256
CODES = 1024
GROUPS = 2
LEVELS = 2
KERNEL = 3
DILATION = 3
DG = 256
COMMIT = 0.25
FIRST_DECAY = 0.9
SECOND_DECAY = 0.99
EPSILON = 1e-08
WEIGHT_DECAY = 0.01
BITRATE_FACTOR = 0.02
RATE_CODE = 0.5


def extended(cells, sides, width):
    for axis, dim in sides:
        count = lax.axis_size(axis)
        ends = count - 1
        head = lax.slice_in_dim(cells, 0, width, axis=dim)
        tail = lax.slice_in_dim(cells, cells.shape[dim] - width, cells.shape[dim], axis=dim)
        cells = jnp.concatenate(
            [
                lax.ppermute(tail, axis, [(i, (i + 1) % count) for i in range(ends)]),
                cells,
                lax.ppermute(head, axis, [((i + 1) % count, i) for i in range(ends)]),
            ],
            axis=dim,
        )
    return cells


def elu_slope(values):
    return jnp.where(values > 0, 1.0, jnp.exp(jnp.minimum(values, 0.0)))


def adamw_update(weight, first, second, grad, rate, completed_steps):
    first_new = FIRST_DECAY * first + (1.0 - FIRST_DECAY) * grad
    second_new = SECOND_DECAY * second + (1.0 - SECOND_DECAY) * grad * grad
    first_hat = first_new / (1.0 - FIRST_DECAY**completed_steps)
    second_hat = second_new / (1.0 - SECOND_DECAY**completed_steps)
    weight_new = weight - rate * (
        first_hat / (jnp.sqrt(second_hat) + EPSILON) + WEIGHT_DECAY * weight
    )
    return (weight_new, grad, second_new)


def shards(
    features,
    cotangent,
    clip_lengths,
    code_ids,
    step_count,
    dilated_kernel_weight,
    pointwise_conv,
    codebooks,
    dilated_first_moment,
    dilated_second_moment,
    pointwise_first,
    pointwise_second,
    codebook_first,
    codebook_second,
):
    clip_rank = lax.axis_index("clip")
    time_rank = lax.axis_index("tm")
    dilated_full, pointwise_full, table_full = (
        lax.all_gather(dilated_kernel_weight.astype(jnp.bfloat16), "clip", axis=2, tiled=True),
        lax.all_gather(pointwise_conv.astype(jnp.bfloat16), "clip", axis=1, tiled=True),
        lax.all_gather(codebooks.astype(jnp.bfloat16), "clip", axis=1, tiled=True),
    )
    clips, frames, width = features.shape
    positions = time_rank * frames + lax.broadcasted_iota(jnp.int32, (clips, frames, 1), 1)
    frame_mask = (positions < clip_lengths[:, None, None]).astype(jnp.float32)
    start = features.astype(jnp.float32) * frame_mask
    activated = jax.nn.elu(start).astype(jnp.bfloat16)
    padded = extended(activated, (("tm", 1),), DILATION)
    hidden = jnp.zeros((clips, frames, HID), jnp.float32)
    for tap_index in range(KERNEL):
        window = padded[:, tap_index * DILATION : tap_index * DILATION + frames]
        hidden = hidden + jnp.einsum(
            "btc,cd->btd", window, dilated_full[tap_index], preferred_element_type=jnp.float32
        )
    gated = jax.nn.elu(hidden).astype(jnp.bfloat16)
    latent = start + jnp.einsum(
        "btk,kd->btd", gated, pointwise_full, preferred_element_type=jnp.float32
    )
    backs = cotangent.astype(jnp.float32) * frame_mask
    latent_parts = []
    quant_parts = []
    table_grads = []
    for group in range(GROUPS):
        residual_part = latent[..., group * DG : (group + 1) * DG]
        moving_grad = backs[..., group * DG : (group + 1) * DG]
        summed = jnp.zeros_like(residual_part)
        for level in range(LEVELS):
            slot = group * LEVELS + level
            chosen = jnp.take(table_full[slot], code_ids[slot], axis=0).astype(jnp.float32)
            moving_grad = moving_grad + 2.0 * COMMIT * frame_mask * (residual_part - chosen)
            code_grad = 2.0 * frame_mask * (chosen - residual_part)
            table_grads.append(
                jax.ops.segment_sum(
                    code_grad.reshape(-1, DG), code_ids[slot].reshape(-1), num_segments=CODES
                )
            )
            residual_part = residual_part - chosen
            summed = summed + chosen
        latent_parts.append(moving_grad)
        quant_parts.append(summed)
    quantized = (jnp.concatenate(quant_parts, axis=-1) * frame_mask).astype(jnp.bfloat16)
    latent_grad = jnp.concatenate(latent_parts, axis=-1)
    table_grad = jnp.stack(table_grads, axis=0)
    branch_grad = latent_grad.astype(jnp.bfloat16)
    pointwise_grad = jnp.einsum(
        "btk,btd->kd", gated, branch_grad, preferred_element_type=jnp.float32
    )
    gated_grad = jnp.einsum(
        "btd,kd->btk", branch_grad, pointwise_full, preferred_element_type=jnp.float32
    )
    hidden_grad = (gated_grad * elu_slope(hidden)).astype(jnp.bfloat16)
    padded_grad = extended(hidden_grad, (("tm", 1),), DILATION)
    dilated_parts = []
    act_grad = jnp.zeros((clips, frames, width), jnp.float32)
    for tap_index in range(KERNEL):
        window = padded[:, tap_index * DILATION : tap_index * DILATION + frames]
        dilated_parts.append(
            jnp.einsum("btc,btd->cd", window, hidden_grad, preferred_element_type=jnp.float32)
        )
        offset = (KERNEL - 1 - tap_index) * DILATION
        act_grad = act_grad + jnp.einsum(
            "btd,cd->btc",
            padded_grad[:, offset : offset + frames],
            dilated_full[tap_index],
            preferred_element_type=jnp.float32,
        )
    dilated_grad = jnp.stack(dilated_parts, axis=0)
    features_gradient = frame_mask * (latent_grad + elu_slope(start) * act_grad)
    local_grads = (dilated_grad, pointwise_grad, table_grad)
    whole = lax.psum((local_grads[0], local_grads[1], local_grads[2]), ("clip", "tm"))
    squared = sum((jnp.sum(piece * piece) for piece in whole))
    shares = (
        lax.dynamic_slice_in_dim(
            whole[0], clip_rank * dilated_kernel_weight.shape[2], dilated_kernel_weight.shape[2], 2
        ),
        lax.dynamic_slice_in_dim(
            whole[1], clip_rank * pointwise_conv.shape[1], pointwise_conv.shape[1], 1
        ),
        lax.dynamic_slice_in_dim(whole[2], clip_rank * codebooks.shape[1], codebooks.shape[1], 1),
    )
    count = dilated_full.size + pointwise_full.size + table_full.size
    limit = jnp.sqrt(jnp.float32(count))
    gradient_norm_total = jnp.sqrt(squared)
    clip_scale_factor = limit / jnp.maximum(gradient_norm_total, limit)
    completed_steps = step_count[0].astype(jnp.float32)
    dilation_factor = adamw_update(
        dilated_kernel_weight,
        dilated_first_moment,
        dilated_second_moment,
        shares[0] * clip_scale_factor,
        BITRATE_FACTOR,
        completed_steps,
    )
    pointwise_kernel = adamw_update(
        pointwise_conv,
        pointwise_first,
        pointwise_second,
        shares[1] * clip_scale_factor,
        BITRATE_FACTOR,
        completed_steps,
    )
    codebook_tensor = adamw_update(
        codebooks,
        codebook_first,
        codebook_second,
        shares[2] * clip_scale_factor,
        RATE_CODE,
        completed_steps,
    )
    return (
        quantized,
        features_gradient,
        gradient_norm_total.reshape(1),
        dilation_factor[0],
        dilation_factor[1],
        dilation_factor[2],
        pointwise_kernel[0],
        pointwise_kernel[1],
        pointwise_kernel[2],
        codebook_tensor[0],
        codebook_tensor[1],
        codebook_tensor[2],
    )


def solution(mesh):
    in_specs = (
        P("clip", "tm", None),
        P("clip", "tm", None),
        P("clip"),
        P(None, "clip", "tm"),
        P(),
        P(None, None, "clip"),
        P(None, "clip"),
        P(None, "clip", None),
        P(None, None, "clip"),
        P(None, None, "clip"),
        P(None, "clip"),
        P(None, "clip"),
        P(None, "clip", None),
        P(None, "clip", None),
    )
    out_specs = (
        P("clip", "tm", None),
        P("clip", "tm", None),
        P(),
        P(None, None, "clip"),
        P(None, None, "clip"),
        P(None, None, "clip"),
        P(None, "clip"),
        P(None, "clip"),
        P(None, "clip"),
        P(None, "clip", None),
        P(None, "clip", None),
        P(None, "clip", None),
    )
    return jax.shard_map(shards, mesh=mesh, in_specs=in_specs, out_specs=out_specs, check_vma=False)
```

profile of v0, /device:TPU:0, one launch (start us, length us, event | category | flops | bytes accessed | tf_op | source)
XLA Modules:
  0.0 310.3 jit_solution(5738353770341371367)
XLA Ops:
  7.2 1.8 convert_element_type.54
  9.8 2.8 convert_multiply_fusion.1
  12.7 1.3 collective-permute-start.1
  14.0 3.0 collective-permute-start
  17.8 0.9 convert_element_type.64
  19.6 33.2 %all_gather.11 = bf16[256,512]{0,1:T(8,128)(2,1)S(1)} all-gather(bf16[256,64]{0,1:T(8,128)(2,1)S(1)} %convert_element_type.66), channel_id=1, replica_groups=mesh['clip'=8,'tm'=4] {'clip'}, dimensions={1}, use_global_device_ids=true | all-gather | bytes 294912 | tf_op jit(solution)/shard_map/all_gather | solution.py:74
  52.9 33.2 %all_gather.10 = bf16[3,512,256]{1,2,0:T(8,128)(2,1)S(1)} all-gather(bf16[3,512,32]{1,2,0:T(8,128)(2,1)S(1)} %convert_element_type.64), channel_id=1, replica_groups=mesh['clip'=8,'tm'=4] {'clip'}, dimensions={2}, use_global_device_ids=true | all-gather | bytes 884736 | tf_op jit(solution)/shard_map/all_gather | solution.py:73
  88.0 1.4 convolution_add_fusion.1
  89.4 1.7 slice_bitcast_fusion.3
  91.1 2.6 gather_fusion.1
  93.7 2.6 gather_fusion
  96.2 2.6 gather_fusion.3
  98.8 1.9 gather_fusion.2
  100.8 3.3 %fusion.12 = (f32[2,256,256]{2,1,0:T(8,128)S(1)}, f32[2,256,256]{2,1,0:T(8,128)S(1)}, f32[2,256,256]{2,1,0:T(8,128)}, f32[2,256,256]{2,1,0:T(8,128)}, f32[2,256,...) fusion(f32[2,256,512]{2,1,0:T(8,128)S(1)} %copy-done, ...), kind=kLoop, calls=%fused_computation.50 | loop fusion | flops 3932160 | bytes 7346176 | tf_op jit(solution)/shard_map/add | solution.py:104
  104.4 1.3 convolution_bitcast_fusion
  106.1 4.2 %scatter_custom_fusion.3 = f32[1024,256]{1,0:T(8,128)S(1)} fusion(s32[512]{0:T(512)S(1)} %bitcast.135, f32[512,256]{1,0:T(8,128)} %bitcast.127, f32[]{:T(128)} %constant.35.clone.1), kind=kCustom, calls=%fused_computation.74 | custom fusion | flops 131072 | bytes 1049088 | tf_op jit(solution)/shard_map/scatter-add | solution.py:107
  110.4 4.8 %scatter_custom_fusion.2 = f32[1024,256]{1,0:T(8,128)} fusion(s32[512]{0:T(512)S(1)} %bitcast.134, f32[512,256]{1,0:T(8,128)} %bitcast.126, f32[]{:T(128)} %constant.35.clone.1), kind=kCustom, calls=%fused_computation.76 | custom fusion | flops 131072 | bytes 1049088 | tf_op jit(solution)/shard_map/scatter-add | solution.py:107
  115.1 4.8 %scatter_custom_fusion.1 = f32[1024,256]{1,0:T(8,128)} fusion(s32[512]{0:T(512)S(1)} %bitcast.133, f32[512,256]{1,0:T(8,128)} %bitcast.125, f32[]{:T(128)} %constant.35.clone.1), kind=kCustom, calls=%fused_computation.78 | custom fusion | flops 131072 | bytes 1049088 | tf_op jit(solution)/shard_map/scatter-add | solution.py:107
  119.9 4.8 %scatter_custom_fusion = f32[1024,256]{1,0:T(8,128)} fusion(s32[512]{0:T(512)S(1)} %bitcast.132, f32[512,256]{1,0:T(8,128)} %bitcast.124, f32[]{:T(128)} %constant.35.clone.1), kind=kCustom, calls=%fused_computation.80 | custom fusion | flops 131072 | bytes 1049088 | tf_op jit(solution)/shard_map/scatter-add | solution.py:107
  125.4 1.3 pad_maximum_fusion.1
  126.8 2.3 pad_maximum_fusion
  130.0 1.4 collective-permute-start.3
  131.4 1.5 collective-permute-start.2
  134.5 1.4 collective-permute-done.2
  136.0 1.6 fusion.3
  137.6 149.0 %all-reduce.3.cloned.1.call-done = (f32[3,512,256]{1,2,0:T(8,128)}, f32[256,512]{0,1:T(8,128)}, f32[4,1024,256]{2,1,0:T(8,128)}) async-done(((f32[3,512,256]{1,2,0:T(8,128)}, f32[256,512]{0,1:T(8,128)}, f32[4,1024,256]{2,1,0:T(8,128)}), (f32[3,512,256]{1,2,0:T(8,128)}, f32[256,512]{0,1:T(8,128)}, f32[4,1024,256]{2,1,0:T(8,128)})) %all-reduce.3.cloned.1.call-update) | async-done | bytes 6291472 | tf_op jit(solution)/shard_map/psum | solution.py:144
  286.6 2.4 multiply_reduce_fusion.1
  289.0 1.8 multiply_reduce_fusion.2
  290.8 3.9 %multiply_reduce_fusion = f32[]{:T(128)} fusion(f32[4,1024,256]{2,1,0:T(8,128)} %get-tuple-element.39), kind=kLoop, calls=%fused_computation.9 | loop fusion | flops 2097151 | bytes 4194308 | tf_op jit(solution)/shard_map/reduce_sum | solution.py:145
  296.7 1.8 multiply_subtract_fusion.1
  298.5 1.5 multiply_subtract_fusion.2
  300.1 2.3 multiply_subtract_fusion
  (93 shorter events, 7.4 us)
Async XLA Ops:
  7.2 45.6 %copy-start.26 = (s32[2]{0:T(128)S(1)}, s32[2]{0:T(128)}, u32[]{:S(2)}) copy-start(s32[2]{0:T(128)} %param.18) | copy-start | bytes 28
  7.2 45.7 %copy-start.23 = (s32[4,2,256]{2,1,0:T(2,128)S(1)}, s32[4,2,256]{2,1,0:T(2,128)}, u32[]{:S(2)}) copy-start(s32[4,2,256]{2,1,0:T(2,128)} %param.19) | copy-start | bytes 24580
  7.2 82.2 %all-gather.2.cloned.1.call-start = ((), (), s32[]{:S(2)}) async-start(), calls=%async_computation | async-start | bytes 2359296 | tf_op jit(solution)/shard_map/all_gather | solution.py:75
  9.0 277.5 %all-reduce.3.cloned.1.call-start = ((), (), s32[]{:S(2)}) async-start(), calls=%async_computation.1 | async-start | bytes 12582912 | tf_op jit(solution)/shard_map/psum | solution.py:144
  9.8 78.2 %copy-start.11 = (bf16[2,256,512]{2,1,0:T(8,128)(2,1)S(1)}, bf16[2,256,512]{2,1,0:T(8,128)(2,1)}, u32[]{:S(2)}) copy-start(bf16[2,256,512]{2,1,0:T(8,128)(2,1)} %param.16) | copy-start | bytes 1572868
  12.7 73.8 %collective-permute-start.1 = (bf16[2,3,512]{2,1,0:T(4,128)(2,1)S(1)}, bf16[2,3,512]{2,1,0:T(4,128)(2,1)S(1)}, u32[]{:S(2)}, u32[]{:S(2)}) collective-permute-start(bf16[2,3,512]{2,1,0:T(4,128)(2,1)S(1)} %get-tuple-element.62), channel_id=1, source_target_pairs={{1,0},{2,1},{3,2},{5,4},{6,5},{7,6},{9,8},{10,9},{11,10},{13,12},{... | collective-permute-start | bytes 18440 | tf_op jit(solution)/shard_map/ppermute | solution.py:32
  14.0 72.9 %collective-permute-start = (bf16[2,3,512]{2,1,0:T(4,128)(2,1)S(1)}, bf16[2,3,512]{2,1,0:T(4,128)(2,1)S(1)}, u32[]{:S(2)}, u32[]{:S(2)}) collective-permute-start(bf16[2,3,512]{2,1,0:T(4,128)(2,1)S(1)} %get-tuple-element.61), channel_id=1, source_target_pairs={{0,1},{1,2},{2,3},{4,5},{5,6},{6,7},{8,9},{9,10},{10,11},{12,13},{... | collective-permute-start | bytes 18440 | tf_op jit(solution)/shard_map/ppermute | solution.py:30
  52.8 34.4 %copy-start.19 = (bf16[256,512]{0,1:T(8,128)(2,1)}, bf16[256,512]{0,1:T(8,128)(2,1)S(1)}, u32[]{:S(2)}) copy-start(bf16[256,512]{0,1:T(8,128)(2,1)S(1)} %all_gather.11) | copy-start | bytes 786436
  96.2 4.5 %copy-start = (f32[2,256,512]{2,1,0:T(8,128)S(1)}, f32[2,256,512]{2,1,0:T(8,128)}, u32[]{:S(2)}) copy-start(f32[2,256,512]{2,1,0:T(8,128)} %get-tuple-element.77) | copy-start | bytes 3145732
  100.8 3.3 %copy-start.17 = (f32[2,256,256]{2,1,0:T(8,128)S(1)}, f32[2,256,256]{2,1,0:T(8,128)}, u32[]{:S(2)}) copy-start(f32[2,256,256]{2,1,0:T(8,128)} %copy-done.16) | copy-start | bytes 1572868
  100.8 3.3 %copy-start.20 = (bf16[256,512]{0,1:T(8,128)(2,1)S(1)}, bf16[256,512]{0,1:T(8,128)(2,1)}, u32[]{:S(2)}) copy-start(bf16[256,512]{0,1:T(8,128)(2,1)} %copy-done.19) | copy-start | bytes 786436
  104.1 2.0 copy-start.7
  104.1 2.0 copy-start.9
  124.7 2.0 copy-start.1
  124.7 2.0 copy-start.2
  124.7 2.0 copy-start.3
  129.0 4.2 %copy-start.5 = (f32[2,256,256]{2,1,0:T(8,128)S(1)}, f32[2,256,256]{2,1,0:T(8,128)}, u32[]{:S(2)}) copy-start(f32[2,256,256]{2,1,0:T(8,128)} %get-tuple-element.59) | copy-start | bytes 1572868
  129.1 4.2 %copy-start.6 = (f32[2,256,256]{2,1,0:T(8,128)S(1)}, f32[2,256,256]{2,1,0:T(8,128)}, u32[]{:S(2)}) copy-start(f32[2,256,256]{2,1,0:T(8,128)} %get-tuple-element.60) | copy-start | bytes 1572868
  129.1 6.9 %copy-start.8 = (f32[2,256,256]{2,1,0:T(8,128)S(1)}, f32[2,256,256]{2,1,0:T(8,128)}, u32[]{:S(2)}) copy-start(f32[2,256,256]{2,1,0:T(8,128)} %copy-done.7) | copy-start | bytes 1572868
  129.1 6.9 %copy-start.10 = (f32[2,256,256]{2,1,0:T(8,128)S(1)}, f32[2,256,256]{2,1,0:T(8,128)}, u32[]{:S(2)}) copy-start(f32[2,256,256]{2,1,0:T(8,128)} %copy-done.9) | copy-start | bytes 1572868
  130.0 6.0 %copy-start.12 = (bf16[2,256,512]{2,1,0:T(8,128)(2,1)S(1)}, bf16[2,256,512]{2,1,0:T(8,128)(2,1)}, u32[]{:S(2)}) copy-start(bf16[2,256,512]{2,1,0:T(8,128)(2,1)} %param.16) | copy-start | bytes 1572868
  130.0 4.2 %collective-permute-start.3 = (bf16[2,3,256]{2,1,0:T(4,128)(2,1)S(1)}, bf16[2,3,256]{2,1,0:T(4,128)(2,1)S(1)}, u32[]{:S(2)}, u32[]{:S(2)}) collective-permute-start(bf16[2,3,256]{2,1,0:T(4,128)(2,1)S(1)} %get-tuple-element.64), channel_id=1, source_target_pairs={{0,1},{1,2},{2,3},{4,5},{5,6},{6,7},{8,9},{9,10},{10,11},{12,13},{... | collective-permute-start | bytes 9224 | tf_op jit(solution)/shard_map/ppermute | solution.py:30
  131.4 4.5 %collective-permute-start.2 = (bf16[2,3,256]{2,1,0:T(4,128)(2,1)S(1)}, bf16[2,3,256]{2,1,0:T(4,128)(2,1)S(1)}, u32[]{:S(2)}, u32[]{:S(2)}) collective-permute-start(bf16[2,3,256]{2,1,0:T(4,128)(2,1)S(1)} %get-tuple-element.63), channel_id=1, source_target_pairs={{1,0},{2,1},{3,2},{5,4},{6,5},{7,6},{9,8},{10,9},{11,10},{13,12},{... | collective-permute-start | bytes 9224 | tf_op jit(solution)/shard_map/ppermute | solution.py:32
  137.5 159.1 %copy-start.13 = (f32[3,512,32]{1,2,0:T(8,128)S(1)}, f32[3,512,32]{1,2,0:T(8,128)}, u32[]{:S(2)}) copy-start(f32[3,512,32]{1,2,0:T(8,128)} %param.21) | copy-start | bytes 589828
  137.5 159.2 %copy-start.21 = (f32[3,512,32]{1,2,0:T(8,128)S(1)}, f32[3,512,32]{1,2,0:T(8,128)}, u32[]{:S(2)}) copy-start(f32[3,512,32]{1,2,0:T(8,128)} %param.24) | copy-start | bytes 589828
  137.5 159.2 %copy-start.22 = (f32[3,512,32]{1,2,0:T(8,128)S(1)}, f32[3,512,32]{1,2,0:T(8,128)}, u32[]{:S(2)}) copy-start(f32[3,512,32]{1,2,0:T(8,128)} %param.25) | copy-start | bytes 589828
  137.5 161.0 %copy-start.18 = (f32[256,64]{0,1:T(8,128)S(1)}, f32[256,64]{0,1:T(8,128)}, u32[]{:S(2)}) copy-start(f32[256,64]{0,1:T(8,128)} %param.22) | copy-start | bytes 196612
  137.5 161.0 %copy-start.24 = (f32[256,64]{0,1:T(8,128)S(1)}, f32[256,64]{0,1:T(8,128)}, u32[]{:S(2)}) copy-start(f32[256,64]{0,1:T(8,128)} %param.26) | copy-start | bytes 196612
  137.5 161.0 %copy-start.25 = (f32[256,64]{0,1:T(8,128)S(1)}, f32[256,64]{0,1:T(8,128)}, u32[]{:S(2)}) copy-start(f32[256,64]{0,1:T(8,128)} %param.27) | copy-start | bytes 196612
  137.6 162.5 %copy-start.4 = (f32[4,128,256]{2,1,0:T(8,128)S(1)}, f32[4,128,256]{2,1,0:T(8,128)}, u32[]{:S(2)}) copy-start(f32[4,128,256]{2,1,0:T(8,128)} %param.23) | copy-start | bytes 1572868
  137.6 162.5 %copy-start.14 = (f32[4,128,256]{2,1,0:T(8,128)S(1)}, f32[4,128,256]{2,1,0:T(8,128)}, u32[]{:S(2)}) copy-start(f32[4,128,256]{2,1,0:T(8,128)} %param.28) | copy-start | bytes 1572868
  137.6 162.5 %copy-start.15 = (f32[4,128,256]{2,1,0:T(8,128)S(1)}, f32[4,128,256]{2,1,0:T(8,128)}, u32[]{:S(2)}) copy-start(f32[4,128,256]{2,1,0:T(8,128)} %param.29) | copy-start | bytes 1572868
  (1 other events, 0.8 us)
Sparse Core Ops, SparseCore 0:
  10.8 58.7 all-gather.1
  129.2 157.3 all-reduce.2
where the time goes:
time: 311 us; the launch traced here: 310 us
  waiting for transfers between devices  150 us (48%)
  blocking collectives  66.4 us (21%)
  other arithmetic  48.1 us (15%)
  between operations  18.6 us (6%)
  local copies, waits for them, and re-layouts  12.2 us (4%)
  starting transfers between devices  7.34 us (2%)
  matrix products  7.32 us (2%)
    psum x1, waiting for transfers between devices, shards(): lax.psum((local_grads[0], local_grads[1], local_grads[2]), ('clip', 'tm'))  149 us
    all_gather x1, blocking collectives, shards(): lax.all_gather(pointwise_conv.astype(jnp.bfloat16), 'clip', axis=1, tiled...  33.2 us
    all_gather x1, blocking collectives, shards(): lax.all_gather(dilated_kernel_weight.astype(jnp.bfloat16), 'clip', axis=2...  33.2 us
    scatter-add x4, other arithmetic, shards(): jax.ops.segment_sum(code_grad.reshape(-1, DG), code_ids[slot].reshape(-1)...  18.6 us
    gather x4, local copies, waits for them, and re-layouts, shards(): jnp.take(table_full[slot], code_ids[slot], axis=0).astype(jnp.float32)  9.65 us
    reduce_sum x3, other arithmetic, shards(): squared = sum((jnp.sum(piece * piece) for piece in whole))  8.06 us
  transfers between devices with their start and end apart: 6, of which 2 were waited for; matrix products, arithmetic and copies ran while one was open for 4% of the time, Pallas kernels for 0%

commit v1 on v0

--- a/solution.py
+++ b/solution.py
@@ -17,6 +17,18 @@
 WEIGHT_DECAY = 0.01
 BITRATE_FACTOR = 0.02
 RATE_CODE = 0.5
+
+
+def collect(x, axis, dim):
+    ways, here, step = (lax.axis_size(axis), lax.axis_index(axis), x.shape[dim])
+    line, have = (x, 1)
+    while have < ways:
+        line = jnp.concatenate(
+            [line, lax.ppermute(line, axis, [(d, (d - have) % ways) for d in range(ways)])],
+            axis=dim,
+        )
+        have = 2 * have
+    return jnp.roll(line, here * step, axis=dim)
 
 
 def extended(cells, sides, width):
@@ -71,7 +83,7 @@
     time_rank = lax.axis_index("tm")
     dilated_full, pointwise_full, table_full = (
         lax.all_gather(dilated_kernel_weight.astype(jnp.bfloat16), "clip", axis=2, tiled=True),
-        lax.all_gather(pointwise_conv.astype(jnp.bfloat16), "clip", axis=1, tiled=True),
+        collect(pointwise_conv.astype(jnp.bfloat16), "clip", 1),
         lax.all_gather(codebooks.astype(jnp.bfloat16), "clip", axis=1, tiled=True),
     )
     clips, frames, width = features.shape

time: 311 us -> 296 us (0.952)
  blocking collectives: 66.4 us -> 33.8 us
  waiting for transfers between devices: 150 us -> 160 us
  starting transfers between devices: 7.34 us -> 14.8 us
    all_gather x1 -> x0, blocking collectives: 33.2 us -> none  [shards(): lax.all_gather(pointwise_conv.astype(jnp.bfloat16), 'clip', axis=1, tiled...]
    ppermute x0 -> x3, waiting for transfers between devices: none -> 12.9 us  [collect(): lax.ppermute(line, axis, [(d, (d - have) % ways) for d in range(ways)])]
    ppermute x0 -> x3, starting transfers between devices: none -> 7.33 us  [collect(): lax.ppermute(line, axis, [(d, (d - have) % ways) for d in range(ways)])]
  transfers between devices with their start and end apart: 6 -> 9, of which waited for: 2 -> 3; matrix products, arithmetic and copies ran while one was open for 4% -> 4% of each run, Pallas kernels for 0% -> 0%
where the time goes in v1:
time: 296 us; the launch traced here: 295 us
  waiting for transfers between devices  160 us (54%)
  other arithmetic  47.4 us (16%)
  blocking collectives  33.8 us (11%)
  between operations  18.6 us (6%)
  starting transfers between devices  14.8 us (5%)
  local copies, waits for them, and re-layouts  12.7 us (4%)
  matrix products  7.5 us (3%)
    psum x1, waiting for transfers between devices, shards(): lax.psum((local_grads[0], local_grads[1], local_grads[2]), ('clip', 'tm'))  147 us
    all_gather x1, blocking collectives, shards(): lax.all_gather(dilated_kernel_weight.astype(jnp.bfloat16), 'clip', axis=2...  33.8 us
    scatter-add x4, other arithmetic, shards(): jax.ops.segment_sum(code_grad.reshape(-1, DG), code_ids[slot].reshape(-1)...  18.6 us
    ppermute x3, waiting for transfers between devices, collect(): lax.ppermute(line, axis, [(d, (d - have) % ways) for d in range(ways)])  12.9 us
    gather x4, local copies, waits for them, and re-layouts, shards(): jnp.take(table_full[slot], code_ids[slot], axis=0).astype(jnp.float32)  9.65 us
    reduce_sum x3, other arithmetic, shards(): squared = sum((jnp.sum(piece * piece) for piece in whole))  8.06 us
    ppermute x3, starting transfers between devices, collect(): lax.ppermute(line, axis, [(d, (d - have) % ways) for d in range(ways)])  7.33 us
  transfers between devices with their start and end apart: 9, of which 3 were waited for; matrix products, arithmetic and copies ran while one was open for 4% of the time, Pallas kernels for 0%

profile of v1, /device:TPU:0, one launch (start us, length us, event | category | flops | bytes accessed | tf_op | source)
XLA Modules:
  0.0 295.0 jit_solution(11265221258972491950)
XLA Ops:
  8.2 6.0 %collective-permute-start.2 = (bf16[256,64]{1,0:T(8,128)(2,1)S(1)}, bf16[256,64]{1,0:T(8,128)(2,1)S(1)}, u32[]{:S(2)}, u32[]{:S(2)}) collective-permute-start(bf16[256,64]{1,0:T(8,128)(2,1)S(1)} %copy.71), channel_id=1, source_target_pairs={{0,28},{4,0},{8,4},{12,8},{16,12},{20,16},{24,20},{28,24},{1,29},{... | collective-permute-start | bytes 98312 | tf_op jit(solution)/shard_map/ppermute | solution.py:27
  14.2 1.8 convert_element_type.54
  16.8 2.7 convert_multiply_fusion.1
  19.6 1.4 collective-permute-start.1
  21.0 3.0 %collective-permute-start = (bf16[2,3,512]{2,1,0:T(4,128)(2,1)S(1)}, bf16[2,3,512]{2,1,0:T(4,128)(2,1)S(1)}, u32[]{:S(2)}, u32[]{:S(2)}) collective-permute-start(bf16[2,3,512]{2,1,0:T(4,128)(2,1)S(1)} %get-tuple-element.61), channel_id=1, source_target_pairs={{0,1},{1,2},{2,3},{4,5},{5,6},{6,7},{8,9},{9,10},{10,11},{12,13},{... | collective-permute-start | bytes 18440 | tf_op jit(solution)/shard_map/ppermute | solution.py:42
  25.9 33.8 %all_gather.7 = bf16[3,512,256]{1,2,0:T(8,128)(2,1)S(1)} all-gather(bf16[3,512,32]{1,2,0:T(8,128)(2,1)S(1)} %convert_element_type.64), channel_id=1, replica_groups=mesh['clip'=8,'tm'=4] {'clip'}, dimensions={2}, use_global_device_ids=true | all-gather | bytes 884736 | tf_op jit(solution)/shard_map/all_gather | solution.py:85
  61.4 5.0 %collective-permute-done.3 = bf16[256,128]{1,0:T(8,128)(2,1)S(1)} collective-permute-done((bf16[256,128]{1,0:T(8,128)(2,1)S(1)}, bf16[256,128]{1,0:T(8,128)(2,1)S(1)}, u32[]{:S(2)}, u32[]{:S(2)}) %collective-permute-start.3) | collective-permute-done | bytes 65568 | tf_op jit(solution)/shard_map/ppermute | solution.py:27
  67.4 7.9 %collective-permute-done.4 = bf16[256,256]{1,0:T(8,128)(2,1)S(1)} collective-permute-done((bf16[256,256]{1,0:T(8,128)(2,1)S(1)}, bf16[256,256]{1,0:T(8,128)(2,1)S(1)}, u32[]{:S(2)}, u32[]{:S(2)}) %collective-permute-start.4) | collective-permute-done | bytes 131104 | tf_op jit(solution)/shard_map/ppermute | solution.py:27
  75.7 1.5 convolution_add_fusion.1
  77.2 1.7 slice_bitcast_fusion.3
  78.9 2.6 gather_fusion.1
  81.4 2.6 gather_fusion
  84.0 2.6 gather_fusion.3
  86.6 1.9 gather_fusion.2
  88.6 3.3 %fusion.12 = (f32[2,256,256]{2,1,0:T(8,128)S(1)}, f32[2,256,256]{2,1,0:T(8,128)S(1)}, f32[2,256,256]{2,1,0:T(8,128)}, f32[2,256,256]{2,1,0:T(8,128)}, f32[2,256,...) fusion(f32[2,256,512]{2,1,0:T(8,128)S(1)} %copy-done, ...), kind=kLoop, calls=%fused_computation.50 | loop fusion | flops 3932160 | bytes 7346176 | tf_op jit(solution)/shard_map/add | solution.py:116
  92.3 1.3 convolution_bitcast_fusion
  94.0 4.2 %scatter_custom_fusion.3 = f32[1024,256]{1,0:T(8,128)S(1)} fusion(s32[512]{0:T(512)S(1)} %bitcast.135, f32[512,256]{1,0:T(8,128)} %bitcast.127, f32[]{:T(128)} %constant.37.clone.1), kind=kCustom, calls=%fused_computation.74 | custom fusion | flops 131072 | bytes 1049088 | tf_op jit(solution)/shard_map/scatter-add | solution.py:119
  98.3 4.8 %scatter_custom_fusion.2 = f32[1024,256]{1,0:T(8,128)} fusion(s32[512]{0:T(512)S(1)} %bitcast.134, f32[512,256]{1,0:T(8,128)} %bitcast.126, f32[]{:T(128)} %constant.37.clone.1), kind=kCustom, calls=%fused_computation.76 | custom fusion | flops 131072 | bytes 1049088 | tf_op jit(solution)/shard_map/scatter-add | solution.py:119
  103.0 4.8 %scatter_custom_fusion.1 = f32[1024,256]{1,0:T(8,128)} fusion(s32[512]{0:T(512)S(1)} %bitcast.133, f32[512,256]{1,0:T(8,128)} %bitcast.125, f32[]{:T(128)} %constant.37.clone.1), kind=kCustom, calls=%fused_computation.78 | custom fusion | flops 131072 | bytes 1049088 | tf_op jit(solution)/shard_map/scatter-add | solution.py:119
  107.9 4.8 %scatter_custom_fusion = f32[1024,256]{1,0:T(8,128)} fusion(s32[512]{0:T(512)S(1)} %bitcast.132, f32[512,256]{1,0:T(8,128)} %bitcast.124, f32[]{:T(128)} %constant.37.clone.1), kind=kCustom, calls=%fused_computation.80 | custom fusion | flops 131072 | bytes 1049088 | tf_op jit(solution)/shard_map/scatter-add | solution.py:119
  113.4 1.3 pad_maximum_fusion.1
  114.7 2.3 pad_maximum_fusion
  117.9 1.4 collective-permute-start.6
  119.4 1.5 collective-permute-start.5
  122.5 1.6 fusion.3
  124.1 147.1 %all-reduce.3.cloned.1.call-done = (f32[3,512,256]{1,2,0:T(8,128)}, f32[256,512]{0,1:T(8,128)}, f32[4,1024,256]{2,1,0:T(8,128)}) async-done(((f32[3,512,256]{1,2,0:T(8,128)}, f32[256,512]{0,1:T(8,128)}, f32[4,1024,256]{2,1,0:T(8,128)}), (f32[3,512,256]{1,2,0:T(8,128)}, f32[256,512]{0,1:T(8,128)}, f32[4,1024,256]{2,1,0:T(8,128)})) %all-reduce.3.cloned.1.call-update) | async-done | bytes 6291472 | tf_op jit(solution)/shard_map/psum | solution.py:156
  271.2 2.4 multiply_reduce_fusion.1
  273.6 1.8 multiply_reduce_fusion.2
  275.4 3.9 %multiply_reduce_fusion = f32[]{:T(128)} fusion(f32[4,1024,256]{2,1,0:T(8,128)} %get-tuple-element.39), kind=kLoop, calls=%fused_computation.9 | loop fusion | flops 2097151 | bytes 4194308 | tf_op jit(solution)/shard_map/reduce_sum | solution.py:157
  281.3 1.8 multiply_subtract_fusion.1
  283.1 1.5 multiply_subtract_fusion.2
  284.7 2.3 multiply_subtract_fusion
  (101 shorter events, 9.6 us)
Async XLA Ops:
  7.2 18.6 %copy-start.26 = (s32[2]{0:T(128)S(1)}, s32[2]{0:T(128)}, u32[]{:S(2)}) copy-start(s32[2]{0:T(128)} %param.18) | copy-start | bytes 28
  7.2 18.7 %copy-start.23 = (s32[4,2,256]{2,1,0:T(2,128)S(1)}, s32[4,2,256]{2,1,0:T(2,128)}, u32[]{:S(2)}) copy-start(s32[4,2,256]{2,1,0:T(2,128)} %param.19) | copy-start | bytes 24580
  7.2 70.0 %all-gather.2.cloned.1.call-start = ((), (), s32[]{:S(2)}) async-start(), calls=%async_computation | async-start | bytes 2359296 | tf_op jit(solution)/shard_map/all_gather | solution.py:87
  8.2 52.0 %collective-permute-start.2 = (bf16[256,64]{1,0:T(8,128)(2,1)S(1)}, bf16[256,64]{1,0:T(8,128)(2,1)S(1)}, u32[]{:S(2)}, u32[]{:S(2)}) collective-permute-start(bf16[256,64]{1,0:T(8,128)(2,1)S(1)} %copy.71), channel_id=1, source_target_pairs={{0,28},{4,0},{8,4},{12,8},{16,12},{20,16},{24,20},{28,24},{1,29},{... | collective-permute-start | bytes 98312 | tf_op jit(solution)/shard_map/ppermute | solution.py:27
  16.0 255.2 %all-reduce.3.cloned.1.call-start = ((), (), s32[]{:S(2)}) async-start(), calls=%async_computation.1 | async-start | bytes 12582912 | tf_op jit(solution)/shard_map/psum | solution.py:156
  19.6 56.1 %copy-start.11 = (bf16[2,256,512]{2,1,0:T(8,128)(2,1)S(1)}, bf16[2,256,512]{2,1,0:T(8,128)(2,1)}, u32[]{:S(2)}) copy-start(bf16[2,256,512]{2,1,0:T(8,128)(2,1)} %param.16) | copy-start | bytes 1572868
  19.6 41.5 %collective-permute-start.1 = (bf16[2,3,512]{2,1,0:T(4,128)(2,1)S(1)}, bf16[2,3,512]{2,1,0:T(4,128)(2,1)S(1)}, u32[]{:S(2)}, u32[]{:S(2)}) collective-permute-start(bf16[2,3,512]{2,1,0:T(4,128)(2,1)S(1)} %get-tuple-element.62), channel_id=1, source_target_pairs={{1,0},{2,1},{3,2},{5,4},{6,5},{7,6},{9,8},{10,9},{11,10},{13,12},{... | collective-permute-start | bytes 18440 | tf_op jit(solution)/shard_map/ppermute | solution.py:44
  21.0 46.0 %collective-permute-start = (bf16[2,3,512]{2,1,0:T(4,128)(2,1)S(1)}, bf16[2,3,512]{2,1,0:T(4,128)(2,1)S(1)}, u32[]{:S(2)}, u32[]{:S(2)}) collective-permute-start(bf16[2,3,512]{2,1,0:T(4,128)(2,1)S(1)} %get-tuple-element.61), channel_id=1, source_target_pairs={{0,1},{1,2},{2,3},{4,5},{5,6},{6,7},{8,9},{9,10},{10,11},{12,13},{... | collective-permute-start | bytes 18440 | tf_op jit(solution)/shard_map/ppermute | solution.py:42
  60.3 6.2 %collective-permute-start.3 = (bf16[256,128]{1,0:T(8,128)(2,1)S(1)}, bf16[256,128]{1,0:T(8,128)(2,1)S(1)}, u32[]{:S(2)}, u32[]{:S(2)}) collective-permute-start(bf16[256,128]{1,0:T(8,128)(2,1)S(1)} %pad_maximum_fusion.14), channel_id=1, source_target_pairs={{0,24},{4,28},{8,0},{12,4},{16,8},{20,12},{24,16},{28,20},{1,25},{... | collective-permute-start | bytes 196616 | tf_op jit(solution)/shard_map/ppermute | solution.py:27
  66.6 8.8 %collective-permute-start.4 = (bf16[256,256]{1,0:T(8,128)(2,1)S(1)}, bf16[256,256]{1,0:T(8,128)(2,1)S(1)}, u32[]{:S(2)}, u32[]{:S(2)}) collective-permute-start(bf16[256,256]{1,0:T(8,128)(2,1)S(1)} %pad_maximum_fusion.13), channel_id=1, source_target_pairs={{0,16},{4,20},{8,24},{12,28},{16,0},{20,4},{24,8},{28,12},{1,17},{... | collective-permute-start | bytes 393224 | tf_op jit(solution)/shard_map/ppermute | solution.py:27
  67.4 9.8 %copy-start.16 = (f32[2,256,256]{2,1,0:T(8,128)}, f32[2,256,256]{2,1,0:T(8,128)S(1)}, u32[]{:S(2)}) copy-start(f32[2,256,256]{2,1,0:T(8,128)S(1)} %get-tuple-element.82) | copy-start | bytes 1572868
  84.0 4.5 %copy-start = (f32[2,256,512]{2,1,0:T(8,128)S(1)}, f32[2,256,512]{2,1,0:T(8,128)}, u32[]{:S(2)}) copy-start(f32[2,256,512]{2,1,0:T(8,128)} %get-tuple-element.77) | copy-start | bytes 3145732
  88.5 3.3 %copy-start.17 = (f32[2,256,256]{2,1,0:T(8,128)S(1)}, f32[2,256,256]{2,1,0:T(8,128)}, u32[]{:S(2)}) copy-start(f32[2,256,256]{2,1,0:T(8,128)} %copy-done.16) | copy-start | bytes 1572868
  88.5 3.3 %copy-start.19 = (bf16[256,1024]{1,0:T(8,128)(2,1)S(1)}, bf16[256,1024]{1,0:T(8,128)(2,1)}, u32[]{:S(2)}) copy-start(bf16[256,1024]{1,0:T(8,128)(2,1)} %copy-done.18) | copy-start | bytes 1572868
  91.8 2.2 copy-start.7
  91.9 2.2 copy-start.9
  117.0 4.2 %copy-start.5 = (f32[2,256,256]{2,1,0:T(8,128)S(1)}, f32[2,256,256]{2,1,0:T(8,128)}, u32[]{:S(2)}) copy-start(f32[2,256,256]{2,1,0:T(8,128)} %get-tuple-element.59) | copy-start | bytes 1572868
  117.0 4.2 %copy-start.6 = (f32[2,256,256]{2,1,0:T(8,128)S(1)}, f32[2,256,256]{2,1,0:T(8,128)}, u32[]{:S(2)}) copy-start(f32[2,256,256]{2,1,0:T(8,128)} %get-tuple-element.60) | copy-start | bytes 1572868
  117.0 5.5 %copy-start.8 = (f32[2,256,256]{2,1,0:T(8,128)S(1)}, f32[2,256,256]{2,1,0:T(8,128)}, u32[]{:S(2)}) copy-start(f32[2,256,256]{2,1,0:T(8,128)} %copy-done.7) | copy-start | bytes 1572868
  117.0 5.5 %copy-start.10 = (f32[2,256,256]{2,1,0:T(8,128)S(1)}, f32[2,256,256]{2,1,0:T(8,128)}, u32[]{:S(2)}) copy-start(f32[2,256,256]{2,1,0:T(8,128)} %copy-done.9) | copy-start | bytes 1572868
  117.9 4.6 %copy-start.12 = (bf16[2,256,512]{2,1,0:T(8,128)(2,1)S(1)}, bf16[2,256,512]{2,1,0:T(8,128)(2,1)}, u32[]{:S(2)}) copy-start(bf16[2,256,512]{2,1,0:T(8,128)(2,1)} %param.16) | copy-start | bytes 1572868
  117.9 4.2 %collective-permute-start.6 = (bf16[2,3,256]{2,1,0:T(4,128)(2,1)S(1)}, bf16[2,3,256]{2,1,0:T(4,128)(2,1)S(1)}, u32[]{:S(2)}, u32[]{:S(2)}) collective-permute-start(bf16[2,3,256]{2,1,0:T(4,128)(2,1)S(1)} %get-tuple-element.64), channel_id=1, source_target_pairs={{0,1},{1,2},{2,3},{4,5},{5,6},{6,7},{8,9},{9,10},{10,11},{12,13},{... | collective-permute-start | bytes 9224 | tf_op jit(solution)/shard_map/ppermute | solution.py:42
  119.4 3.1 %collective-permute-start.5 = (bf16[2,3,256]{2,1,0:T(4,128)(2,1)S(1)}, bf16[2,3,256]{2,1,0:T(4,128)(2,1)S(1)}, u32[]{:S(2)}, u32[]{:S(2)}) collective-permute-start(bf16[2,3,256]{2,1,0:T(4,128)(2,1)S(1)} %get-tuple-element.63), channel_id=1, source_target_pairs={{1,0},{2,1},{3,2},{5,4},{6,5},{7,6},{9,8},{10,9},{11,10},{13,12},{... | collective-permute-start | bytes 9224 | tf_op jit(solution)/shard_map/ppermute | solution.py:44
  124.1 157.2 %copy-start.13 = (f32[3,512,32]{1,2,0:T(8,128)S(1)}, f32[3,512,32]{1,2,0:T(8,128)}, u32[]{:S(2)}) copy-start(f32[3,512,32]{1,2,0:T(8,128)} %param.21) | copy-start | bytes 589828
  124.1 157.2 %copy-start.21 = (f32[3,512,32]{1,2,0:T(8,128)S(1)}, f32[3,512,32]{1,2,0:T(8,128)}, u32[]{:S(2)}) copy-start(f32[3,512,32]{1,2,0:T(8,128)} %param.24) | copy-start | bytes 589828
  124.1 157.2 %copy-start.22 = (f32[3,512,32]{1,2,0:T(8,128)S(1)}, f32[3,512,32]{1,2,0:T(8,128)}, u32[]{:S(2)}) copy-start(f32[3,512,32]{1,2,0:T(8,128)} %param.25) | copy-start | bytes 589828
  124.1 159.1 %copy-start.20 = (f32[256,64]{0,1:T(8,128)S(1)}, f32[256,64]{0,1:T(8,128)}, u32[]{:S(2)}) copy-start(f32[256,64]{0,1:T(8,128)} %param.22) | copy-start | bytes 196612
  124.1 159.1 %copy-start.24 = (f32[256,64]{0,1:T(8,128)S(1)}, f32[256,64]{0,1:T(8,128)}, u32[]{:S(2)}) copy-start(f32[256,64]{0,1:T(8,128)} %param.26) | copy-start | bytes 196612
  124.1 159.0 %copy-start.25 = (f32[256,64]{0,1:T(8,128)S(1)}, f32[256,64]{0,1:T(8,128)}, u32[]{:S(2)}) copy-start(f32[256,64]{0,1:T(8,128)} %param.27) | copy-start | bytes 196612
  124.1 160.6 %copy-start.4 = (f32[4,128,256]{2,1,0:T(8,128)S(1)}, f32[4,128,256]{2,1,0:T(8,128)}, u32[]{:S(2)}) copy-start(f32[4,128,256]{2,1,0:T(8,128)} %param.23) | copy-start | bytes 1572868
  124.1 160.6 %copy-start.14 = (f32[4,128,256]{2,1,0:T(8,128)S(1)}, f32[4,128,256]{2,1,0:T(8,128)}, u32[]{:S(2)}) copy-start(f32[4,128,256]{2,1,0:T(8,128)} %param.28) | copy-start | bytes 1572868
  124.1 160.6 %copy-start.15 = (f32[4,128,256]{2,1,0:T(8,128)S(1)}, f32[4,128,256]{2,1,0:T(8,128)}, u32[]{:S(2)}) copy-start(f32[4,128,256]{2,1,0:T(8,128)} %param.29) | copy-start | bytes 1572868
  (4 other events, 7.7 us)
Sparse Core Ops, SparseCore 0:
  16.1 57.4 all-gather.1
  117.2 153.9 all-reduce.2
